TPU v7x, 32 devices: a whole 2x2x4 slice. The times are simulated.
32 devices in a mesh: energy: 4 (over z), rows: 8 (over y, x, core).
Axes of the slice: x: 2, y: 2, z: 4, core: 2. Of those that a mesh axis runs over, the one named last changes fastest.
Arguments:
- coupling: bfloat16 [2, 512, 512], replicated, may hold values from -4.1875 to 4.1875
- inverses: bfloat16 [32, 4, 2, 256, 256], P(('energy', 'rows')), may hold values from -0.0078125 to 0.0078125
- contact_row: int32 [12], replicated, may hold values from 0 to 7, as said below
- assignment: int32 [8], P('energy'), may hold values from 0 to 7, as said below
- states: bfloat16 [12, 2, 16, 512], replicated, may hold values from -0.119628906 to 0.119628906
- weights: float32 [8], P('energy'), may hold values from 0.03 to 0.3
Outputs:
- injection: float32 [8, 8, 2, 16, 512], P('energy', 'rows')
- integrated: float32 [8, 2, 16, 512], P('rows')
- far_forward: bfloat16 [32, 2, 256, 256], P(('energy', 'rows'))
- far_backward: bfloat16 [32, 2, 256, 256], P(('energy', 'rows'))
Inputs may be any that keep to these rules, and one draw needn't show every extreme that they name: `contact_row`: every device block row has one contact or more. `assignment`: each aligned block of 2 entries, b * 2 to b * 2 + 1, holds each of those same numbers once.
All inputs are finite; a program needn't handle non-finite values.
Results may differ from a plain program's by a relative error of at most 0.024.
Values may be sent and summed in bfloat16 or wider, within the bound.
A program may use at most 64 MiB of HBM per device.

v0:
```python
import jax
import jax.numpy as jnp
from jax import lax
from jax.sharding import PartitionSpec as P

ITERS = 4
ROWS_DEV = 1


def partner(shard, axis, stride):
    return lax.ppermute(shard, axis, [(i, i ^ 1 << stride) for i in range(lax.axis_size(axis))])


def single(leading, trailing):
    return jnp.dot(leading, trailing, preferred_element_type=jnp.float32)


def paired_dot(first_left, first_right, second_left, second_right):
    real_part = (
        single(first_left[0], first_right[0])
        - single(first_left[1], first_right[1])
        + single(second_left[0], second_right[0])
        - single(second_left[1], second_right[1])
    )
    imag_part = (
        single(first_left[0], first_right[1])
        + single(first_left[1], first_right[0])
        + single(second_left[0], second_right[1])
        + single(second_left[1], second_right[0])
    )
    return jnp.stack([real_part, imag_part])


def block_product(own_left, other_left, own_right, other_right, row_bit, column_bit):

    def aligned():
        return paired_dot(own_left, own_right, other_left, other_right)

    def crossed():
        return paired_dot(own_left, other_right, other_left, own_right)

    return lax.cond(row_bit == column_bit, aligned, crossed)


def quarter(matrix, row_half, column_half, half_order):
    return lax.dynamic_slice(
        matrix,
        (jnp.int32(0), row_half * half_order, column_half * half_order),
        (2, half_order, half_order),
    )


def local(coupling, inverses, contact_row, assignment, states, weights):
    position = lax.axis_index("rows")
    row_bit = position // 2 % 2
    column_bit = position % 2
    half_order = inverses.shape[-1]
    forward = quarter(coupling, row_bit, column_bit, half_order)
    mirror = quarter(coupling, column_bit, row_bit, half_order)
    backward = jnp.stack([mirror[0].T, -mirror[1].T])
    surface_sum = jnp.zeros((2, half_order, half_order), jnp.float32)
    for iteration in range(ITERS):
        inverse = inverses[0, iteration]
        forward_far, backward_far = partner((forward, backward), "rows", 0)
        inverse_down, forward_down, backward_down = partner((inverse, forward, backward), "rows", 1)
        forward_green = block_product(
            forward, forward_far, inverse, inverse_down, row_bit, column_bit
        ).astype(jnp.bfloat16)
        backward_green = block_product(
            backward, backward_far, inverse, inverse_down, row_bit, column_bit
        ).astype(jnp.bfloat16)
        forward_green_far, backward_green_far = partner((forward_green, backward_green), "rows", 0)
        surface_sum = surface_sum + block_product(
            forward_green, forward_green_far, backward, backward_down, row_bit, column_bit
        )
        forward_next = block_product(
            forward_green, forward_green_far, forward, forward_down, row_bit, column_bit
        ).astype(jnp.bfloat16)
        backward = block_product(
            backward_green, backward_green_far, backward, backward_down, row_bit, column_bit
        ).astype(jnp.bfloat16)
        forward = forward_next
    self_energy = surface_sum.astype(jnp.bfloat16)
    groups = assignment.shape[0]
    states_count = states.shape[2]
    contacts = contact_row.shape[0]
    flat_states = states.reshape(contacts, -1)
    block_rows = ROWS_DEV * lax.axis_size("rows")
    row_ids = jnp.arange(block_rows, dtype=jnp.int32)
    selector = (contact_row[None, :] == row_ids[:, None]).astype(jnp.bfloat16)
    drive = jnp.dot(selector, flat_states, preferred_element_type=jnp.float32).astype(jnp.bfloat16)
    drive = drive.reshape(block_rows, 2, states_count, 2, half_order)
    drive_half = lax.dynamic_index_in_dim(drive, column_bit, axis=3, keepdims=False)

    def contract_own(energy_part, drive_part):
        return jnp.einsum(
            "mn,rkn->rkm", energy_part, drive_part, preferred_element_type=jnp.float32
        )

    real_part = contract_own(self_energy[0], drive_half[:, 0]) - contract_own(
        self_energy[1], drive_half[:, 1]
    )
    imag_part = contract_own(self_energy[0], drive_half[:, 1]) + contract_own(
        self_energy[1], drive_half[:, 0]
    )
    partial_terms = jnp.stack([real_part, imag_part], axis=1)
    received = lax.all_to_all(
        partial_terms[:, None].astype(jnp.bfloat16), "rows", split_axis=0, concat_axis=1, tiled=True
    ).astype(jnp.float32)
    summed = received.reshape(ROWS_DEV, groups, 2, 2, 2, states_count, half_order).sum(axis=3)
    slots = summed.transpose(1, 0, 3, 4, 2, 5).reshape(
        groups, ROWS_DEV, 2, states_count, 2 * half_order
    )
    local_slot = assignment % groups
    slot_index = jnp.arange(groups, dtype=jnp.int32)
    source_slot = jnp.sum(
        jnp.where(local_slot[None, :] == slot_index[:, None], slot_index[None, :], 0), axis=1
    )
    injection = jnp.take(slots, source_slot, axis=0)
    weighted = jnp.tensordot(weights, injection, axes=1, precision=lax.Precision.HIGHEST)
    integrated = lax.psum(weighted.astype(jnp.bfloat16), "energy").astype(jnp.float32)
    return (injection, integrated, forward[None], backward[None])


def solution(mesh):
    placed = (
        P(),
        P(("energy", "rows"), None, None, None, None),
        P(),
        P("energy"),
        P(),
        P("energy"),
    )
    return jax.shard_map(
        local,
        mesh=mesh,
        in_specs=placed,
        out_specs=(
            P("energy", "rows", None, None, None),
            P("rows", None, None, None),
            P(("energy", "rows"), None, None, None),
            P(("energy", "rows"), None, None, None),
        ),
        check_vma=False,
    )
```

profile of v0, /device:TPU:0, one launch (start us, length us, event | category | flops | bytes accessed | tf_op | source)
XLA Modules:
  0.0 174.6 jit_solution(10024723884173628811)
XLA Ops:
  1.7 3.0 %collective-permute-start.4 = (bf16[2,256,256]{2,1,0:T(8,128)(2,1)S(1)}, bf16[2,256,256]{2,1,0:T(8,128)(2,1)S(1)}, u32[]{:S(2)}, u32[]{:S(2)}) collective-permute-start(bf16[2,256,256]{2,1,0:T(8,128)(2,1)S(1)} %constant_dynamic-slice_fusion.1), channel_id=1, source_target_pairs={{0,2},{1,3},{2,0},{3,1},{4,6},{5,7},{6,4},{7,5},{8,10},{9,11},{10,... | collective-permute-start | bytes 786440 | tf_op jit(solution)/shard_map/ppermute | solution.py:11
  4.7 1.3 slice_bitcast_fusion
  7.9 8.7 %collective-permute-done = bf16[2,256,256]{2,1,0:T(8,128)(2,1)S(1)} collective-permute-done((bf16[2,256,256]{2,1,0:T(8,128)(2,1)S(1)}, bf16[2,256,256]{2,1,0:T(8,128)(2,1)S(1)}, u32[]{:S(2)}, u32[]{:S(2)}) %collective-permute-start) | collective-permute-done | bytes 262176 | tf_op jit(solution)/shard_map/ppermute | solution.py:11
  16.6 1.6 conditional.100
  18.3 1.8 %collective-permute-start.2 = (bf16[2,256,256]{2,1,0:T(8,128)(2,1)S(1)}, bf16[2,256,256]{2,1,0:T(8,128)(2,1)}, u32[]{:S(2)}, u32[]{:S(2)}) collective-permute-start(bf16[2,256,256]{2,1,0:T(8,128)(2,1)S(1)} %pad_maximum_fusion.40), channel_id=1, source_target_pairs={{0,2},{1,3},{2,0},{3,1},{4,6},{5,7},{6,4},{7,5},{8,10},{9,11},{10,... | collective-permute-start | bytes 786440 | tf_op jit(solution)/shard_map/ppermute | solution.py:11
  20.4 1.6 conditional.104
  22.1 1.6 conditional.102
  24.2 1.8 %collective-permute-start.11 = (bf16[2,256,256]{2,1,0:T(8,128)(2,1)S(1)}, bf16[2,256,256]{2,1,0:T(8,128)(2,1)}, u32[]{:S(2)}, u32[]{:S(2)}) collective-permute-start(bf16[2,256,256]{2,1,0:T(8,128)(2,1)S(1)} %get-tuple-element.680), channel_id=1, source_target_pairs={{0,2},{1,3},{2,0},{3,1},{4,6},{5,7},{6,4},{7,5},{8,10},{9,11},{10,... | collective-permute-start | bytes 786440 | tf_op jit(solution)/shard_map/ppermute | solution.py:11
  26.0 1.7 collective-permute-done.2
  27.6 5.2 %conditional.105 = (bf16[2,256,256]{2,1,0:T(8,128)(2,1)S(1)}) conditional(s32[]{:T(128)} %convert_element_type.223, (bf16[2,256,256]{2,1,0:T(8,128)(2,1)S(1)}, bf16[2,256,256]{2,1,0:T(8,128)(2,1)}, bf16[2,256,256]{2,1,0:T(8,128)(2,1)S(1)}, bf16[256,256]{1,0:T(8,128)(2,1)S(1)}, bf16[256,256]{1,0:T(8,128)(2,1)S(1)}) %tuple.379, ...), branch_computations={%region_11.12_spmd, %region_12.13_spmd} | conditional | flops 269090816 | bytes 6029320
  33.1 1.6 conditional.103
  35.1 1.8 %collective-permute-start.12 = (bf16[2,256,256]{2,1,0:T(8,128)(2,1)S(1)}, bf16[2,256,256]{2,1,0:T(8,128)(2,1)S(1)}, u32[]{:S(2)}, u32[]{:S(2)}) collective-permute-start(bf16[2,256,256]{2,1,0:T(8,128)(2,1)S(1)} %get-tuple-element.675), channel_id=1, source_target_pairs={{0,2},{1,3},{2,0},{3,1},{4,6},{5,7},{6,4},{7,5},{8,10},{9,11},{10,... | collective-permute-start | bytes 786440 | tf_op jit(solution)/shard_map/ppermute | solution.py:11
  37.1 1.6 conditional.109
  38.8 5.2 %conditional.107 = (bf16[2,256,256]{2,1,0:T(8,128)(2,1)S(1)}) conditional(s32[]{:T(128)} %convert_element_type.223, (bf16[2,256,256]{2,1,0:T(8,128)(2,1)S(1)}, bf16[2,256,256]{2,1,0:T(8,128)(2,1)}, bf16[2,256,256]{2,1,0:T(8,128)(2,1)S(1)}, bf16[2,256,256]{2,1,0:T(8,128)(2,1)S(1)}) %tuple.302, (bf16[2,256,256]{2,1,0:T(8,128)(2,1)S(1)}, ...), branch_computations={%region_15.16_spmd, %region_16.17_spmd} | conditional | flops 269090816 | bytes 6029320
  44.5 1.8 %collective-permute-start.18 = (bf16[2,256,256]{2,1,0:T(8,128)(2,1)S(1)}, bf16[2,256,256]{2,1,0:T(8,128)(2,1)}, u32[]{:S(2)}, u32[]{:S(2)}) collective-permute-start(bf16[2,256,256]{2,1,0:T(8,128)(2,1)S(1)} %get-tuple-element.685), channel_id=1, source_target_pairs={{0,2},{1,3},{2,0},{3,1},{4,6},{5,7},{6,4},{7,5},{8,10},{9,11},{10,... | collective-permute-start | bytes 786440 | tf_op jit(solution)/shard_map/ppermute | solution.py:11
  46.3 3.7 %collective-permute-done.9 = bf16[2,256,256]{2,1,0:T(8,128)(2,1)} collective-permute-done((bf16[2,256,256]{2,1,0:T(8,128)(2,1)S(1)}, bf16[2,256,256]{2,1,0:T(8,128)(2,1)}, u32[]{:S(2)}, u32[]{:S(2)}) %collective-permute-start.9) | collective-permute-done | bytes 262176 | tf_op jit(solution)/shard_map/ppermute | solution.py:11
  50.0 5.2 %conditional.110 = (bf16[2,256,256]{2,1,0:T(8,128)(2,1)S(1)}) conditional(s32[]{:T(128)} %convert_element_type.223, (bf16[2,256,256]{2,1,0:T(8,128)(2,1)S(1)}, bf16[2,256,256]{2,1,0:T(8,128)(2,1)}, bf16[2,256,256]{2,1,0:T(8,128)(2,1)S(1)}, bf16[2,256,256]{2,1,0:T(8,128)(2,1)S(1)}) %tuple.308, (bf16[2,256,256]{2,1,0:T(8,128)(2,1)S(1)}, ...), branch_computations={%region_21.22_spmd, %region_22.23_spmd} | conditional | flops 269090816 | bytes 6029320
  55.3 5.4 %conditional.108 = (bf16[2,256,256]{2,1,0:T(8,128)(2,1)S(1)}) conditional(s32[]{:T(128)} %convert_element_type.223, (bf16[2,256,256]{2,1,0:T(8,128)(2,1)S(1)}, bf16[2,256,256]{2,1,0:T(8,128)(2,1)S(1)}, bf16[2,256,256]{2,1,0:T(8,128)(2,1)}, bf16[2,256,256]{2,1,0:T(8,128)(2,1)S(1)}) %tuple.304, (bf16[2,256,256]{2,1,0:T(8,128)(2,1)S(1)}, ...), branch_computations={%region_17.18_spmd, %region_18.19_spmd} | conditional | flops 269090816 | bytes 6029320
  61.2 1.6 collective-permute-start.19
  65.6 2.0 %convolution_convert_fusion = bf16[8,16384]{1,0:T(8,128)(2,1)} fusion(bf16[12,16384]{1,0:T(8,128)(2,1)} %bitcast.1814, s32[12]{0:T(128)S(1)} %copy-done.4), kind=kOutput, calls=%fused_computation.1673 | convolution fusion | flops 3276896 | bytes 655408 | tf_op jit(solution)/shard_map/dot_general | solution.py:91
  68.0 5.9 %conditional.114 = (bf16[2,256,256]{2,1,0:T(8,128)(2,1)}) conditional(s32[]{:T(128)} %convert_element_type.223, (bf16[2,256,256]{2,1,0:T(8,128)(2,1)S(1)}, bf16[2,256,256]{2,1,0:T(8,128)(2,1)S(1)}, bf16[2,256,256]{2,1,0:T(8,128)(2,1)}, bf16[2,256,256]{2,1,0:T(8,128)(2,1)S(1)}) %tuple.316, (bf16[2,256,256]{2,1,0:T(8,128)(2,1)S(1)}, ...), branch_computations={%region_29.30_spmd, %region_30.31_spmd} | conditional | flops 269090816 | bytes 6029320
  73.9 5.5 %conditional.112 = (bf16[2,256,256]{2,1,0:T(8,128)(2,1)S(1)}) conditional(s32[]{:T(128)} %convert_element_type.223, (bf16[2,256,256]{2,1,0:T(8,128)(2,1)S(1)}, bf16[2,256,256]{2,1,0:T(8,128)(2,1)}, bf16[2,256,256]{2,1,0:T(8,128)(2,1)}, bf16[2,256,256]{2,1,0:T(8,128)(2,1)S(1)}) %tuple.312, (bf16[2,256,256]{2,1,0:T(8,128)(2,1)S(1)}, ...), branch_computations={%region_25.26_spmd, %region_26.27_spmd} | conditional | flops 269090816 | bytes 6029320
  75.4 1.2 fusion.852
  79.3 3.9 %collective-permute-start.20 = (bf16[2,256,256]{2,1,0:T(8,128)(2,1)S(1)}, bf16[2,256,256]{2,1,0:T(8,128)(2,1)S(1)}, u32[]{:S(2)}, u32[]{:S(2)}) collective-permute-start(bf16[2,256,256]{2,1,0:T(8,128)(2,1)S(1)} %get-tuple-element.690), channel_id=1, source_target_pairs={{0,1},{1,0},{2,3},{3,2},{4,5},{5,4},{6,7},{7,6},{8,9},{9,8},{10,11... | collective-permute-start | bytes 786440 | tf_op jit(solution)/shard_map/ppermute | solution.py:11
  83.3 1.6 constant_dynamic-slice_fusion.2
  84.9 9.1 %conditional.115 = (bf16[2,256,256]{2,1,0:T(8,128)(2,1)S(1)}) conditional(s32[]{:T(128)} %convert_element_type.223, (bf16[2,256,256]{2,1,0:T(8,128)(2,1)}, bf16[2,256,256]{2,1,0:T(8,128)(2,1)}, bf16[2,256,256]{2,1,0:T(8,128)(2,1)}, bf16[2,256,256]{2,1,0:T(8,128)(2,1)S(1)}) %tuple.318, (bf16[2,256,256]{2,1,0:T(8,128)(2,1)}, ...), branch_computations={%region_31.32_spmd, %region_32.33_spmd} | conditional | flops 269090816 | bytes 6029320
  87.1 1.2 convolution_add_fusion.125
  88.3 1.2 fusion.1068
  91.6 1.2 convolution_add_fusion.127
  94.1 1.6 collective-permute-start.23
  95.6 1.6 conditional.113
  98.4 5.2 %conditional.101 = (f32[2,256,256]{2,1,0:T(8,128)S(1)}) conditional(s32[]{:T(128)} %convert_element_type.223, (bf16[2,256,256]{2,1,0:T(8,128)(2,1)S(1)}, bf16[2,256,256]{2,1,0:T(8,128)(2,1)}, bf16[2,256,256]{2,1,0:T(8,128)(2,1)S(1)}, bf16[256,256]{1,0:T(8,128)(2,1)S(1)}, bf16[256,256]{1,0:T(8,128)(2,1)S(1)}) %tuple.381, ...), branch_computations={%region_3.4_spmd, %region_4.5_spmd} | conditional | flops 268959744 | bytes 6815752 | solution.py:42
  103.6 5.2 %conditional.106 = (f32[2,256,256]{2,1,0:T(8,128)S(1)}) conditional(s32[]{:T(128)} %convert_element_type.223, (bf16[2,256,256]{2,1,0:T(8,128)(2,1)S(1)}, bf16[2,256,256]{2,1,0:T(8,128)(2,1)}, bf16[2,256,256]{2,1,0:T(8,128)(2,1)S(1)}, bf16[2,256,256]{2,1,0:T(8,128)(2,1)S(1)}) %tuple.300, (bf16[2,256,256]{2,1,0:T(8,128)(2,1)S(1)}, ...), branch_computations={%region_13.14_spmd, %region_14.15_spmd} | conditional | flops 268959744 | bytes 6815752 | solution.py:42
  109.5 6.3 %conditional.111 = (f32[2,256,256]{2,1,0:T(8,128)}) conditional(s32[]{:T(128)} %convert_element_type.223, (bf16[2,256,256]{2,1,0:T(8,128)(2,1)S(1)}, bf16[2,256,256]{2,1,0:T(8,128)(2,1)}, bf16[2,256,256]{2,1,0:T(8,128)(2,1)}, bf16[2,256,256]{2,1,0:T(8,128)(2,1)S(1)}) %tuple.310, (bf16[2,256,256]{2,1,0:T(8,128)(2,1)S(1)}, ...), branch_computations={%region_23.24_spmd, %region_24.25_spmd} | conditional | flops 268959744 | bytes 6815752 | solution.py:42
  109.9 1.2 convolution_add_fusion.93
  111.1 1.2 fusion.780
  112.6 1.2 convolution_add_fusion.95
  113.8 1.2 fusion.781
  115.8 5.2 %conditional.118 = (bf16[2,256,256]{2,1,0:T(8,128)(2,1)S(1)}) conditional(s32[]{:T(128)} %convert_element_type.223, (bf16[2,256,256]{2,1,0:T(8,128)(2,1)S(1)}, bf16[2,256,256]{2,1,0:T(8,128)(2,1)S(1)}, bf16[2,256,256]{2,1,0:T(8,128)(2,1)}, bf16[2,256,256]{2,1,0:T(8,128)(2,1)S(1)}) %tuple.324, (bf16[2,256,256]{2,1,0:T(8,128)(2,1)S(1)}, ...), branch_computations={%region_39.40_spmd, %region_40.41_spmd} | conditional | flops 269090816 | bytes 6029320
  121.0 3.5 %collective-permute-start.27 = (bf16[2,256,256]{2,1,0:T(8,128)(2,1)S(1)}, bf16[2,256,256]{2,1,0:T(8,128)(2,1)S(1)}, u32[]{:S(2)}, u32[]{:S(2)}) collective-permute-start(bf16[2,256,256]{2,1,0:T(8,128)(2,1)S(1)} %get-tuple-element.696), channel_id=1, source_target_pairs={{0,1},{1,0},{2,3},{3,2},{4,5},{5,4},{6,7},{7,6},{8,9},{9,8},{10,11... | collective-permute-start | bytes 786440 | tf_op jit(solution)/shard_map/ppermute | solution.py:11
  124.5 6.5 %conditional.116 = (f32[2,256,256]{2,1,0:T(8,128)}) conditional(s32[]{:T(128)} %convert_element_type.223, (bf16[2,256,256]{2,1,0:T(8,128)(2,1)S(1)}, bf16[2,256,256]{2,1,0:T(8,128)(2,1)}, bf16[2,256,256]{2,1,0:T(8,128)(2,1)}, bf16[2,256,256]{2,1,0:T(8,128)(2,1)S(1)}) %tuple.320, (bf16[2,256,256]{2,1,0:T(8,128)(2,1)S(1)}, ...), branch_computations={%region_33.34_spmd, %region_34.35_spmd} | conditional | flops 268959744 | bytes 6815752 | solution.py:42
  126.3 1.2 fusion.1140
  127.9 1.2 convolution_add_fusion.135
  131.0 1.2 add_convert_fusion
  133.7 6.9 %all-to-all-start = ((bf16[8,1,2,16,256]{4,3,2,1,0:T(8,128)(2,1)}), bf16[8,1,2,16,256]{4,3,2,1,0:T(8,128)(2,1)S(1)}, u32[]{:S(2)}, u32[]{:S(2)}) async-start(bf16[8,1,2,16,256]{4,3,2,1,0:T(8,128)(2,1)} %copy.23), calls=%async_computation | async-start | bytes 262144 | tf_op jit(solution)/shard_map/all_to_all | solution.py:107
  140.6 5.2 %conditional.117 = (bf16[1,2,256,256]{3,2,1,0:T(8,128)(2,1)S(1)}) conditional(s32[]{:T(128)} %convert_element_type.223, (bf16[2,256,256]{2,1,0:T(8,128)(2,1)S(1)}, bf16[2,256,256]{2,1,0:T(8,128)(2,1)S(1)}, bf16[2,256,256]{2,1,0:T(8,128)(2,1)}, bf16[2,256,256]{2,1,0:T(8,128)(2,1)S(1)}) %tuple.322, (bf16[2,256,256]{2,1,0:T(8,128)(2,1)S(1)}, ...), branch_computations={%region_37.38_spmd, %region_38.39_spmd} | conditional | flops 269090816 | bytes 6029320
  146.5 5.2 %conditional.119 = (bf16[1,2,256,256]{3,2,1,0:T(8,128)(2,1)S(1)}) conditional(s32[]{:T(128)} %convert_element_type.223, (bf16[2,256,256]{2,1,0:T(8,128)(2,1)S(1)}, bf16[2,256,256]{2,1,0:T(8,128)(2,1)}, bf16[2,256,256]{2,1,0:T(8,128)(2,1)S(1)}, bf16[2,256,256]{2,1,0:T(8,128)(2,1)S(1)}) %tuple.326, (bf16[2,256,256]{2,1,0:T(8,128)(2,1)S(1)}, ...), branch_computations={%region_41.42_spmd, %region_42.43_spmd} | conditional | flops 269090816 | bytes 6029320
  154.7 19.3 %psum.7 = bf16[1,2,16,512]{3,2,1,0:T(8,128)(2,1)S(1)} all-reduce(bf16[1,2,16,512]{3,2,1,0:T(8,128)(2,1)S(1)} %copy.44), channel_id=1, replica_groups=mesh['energy'=4,'rows'=8] {'energy'}, use_global_device_ids=true, to_apply=%region_36.37 | all-reduce | flops 16384 | bytes 65536 | tf_op jit(solution)/shard_map/psum | solution.py:121
  (257 shorter events, 93.2 us)
Async XLA Ops:
  0.6 153.4 %copy-start = (f32[2]{0:T(128)S(1)}, f32[2]{0:T(128)}, u32[]{:S(2)}) copy-start(f32[2]{0:T(128)} %param.51) | copy-start | bytes 28
  1.7 20.4 %collective-permute-start.4 = (bf16[2,256,256]{2,1,0:T(8,128)(2,1)S(1)}, bf16[2,256,256]{2,1,0:T(8,128)(2,1)S(1)}, u32[]{:S(2)}, u32[]{:S(2)}) collective-permute-start(bf16[2,256,256]{2,1,0:T(8,128)(2,1)S(1)} %constant_dynamic-slice_fusion.1), channel_id=1, source_target_pairs={{0,2},{1,3},{2,0},{3,1},{4,6},{5,7},{6,4},{7,5},{8,10},{9,11},{10,... | collective-permute-start | bytes 786440 | tf_op jit(solution)/shard_map/ppermute | solution.py:11
  4.7 3.2 %collective-permute-start.1 = (bf16[2,256,256]{2,1,0:T(8,128)(2,1)S(1)}, bf16[2,256,256]{2,1,0:T(8,128)(2,1)S(1)}, u32[]{:S(2)}, u32[]{:S(2)}) collective-permute-start(bf16[2,256,256]{2,1,0:T(8,128)(2,1)S(1)} %constant_dynamic-slice_fusion.1), channel_id=1, source_target_pairs={{0,1},{1,0},{2,3},{3,2},{4,5},{5,4},{6,7},{7,6},{8,9},{9,8},{10,11... | collective-permute-start | bytes 786440 | tf_op jit(solution)/shard_map/ppermute | solution.py:11
  6.0 10.7 %collective-permute-start = (bf16[2,256,256]{2,1,0:T(8,128)(2,1)S(1)}, bf16[2,256,256]{2,1,0:T(8,128)(2,1)S(1)}, u32[]{:S(2)}, u32[]{:S(2)}) collective-permute-start(bf16[2,256,256]{2,1,0:T(8,128)(2,1)S(1)} %get-tuple-element.674), channel_id=1, source_target_pairs={{0,2},{1,3},{2,0},{3,1},{4,6},{5,7},{6,4},{7,5},{8,10},{9,11},{10,... | collective-permute-start | bytes 786440 | tf_op jit(solution)/shard_map/ppermute | solution.py:11
  7.4 13.0 %collective-permute-start.7 = (bf16[2,256,256]{2,1,0:T(8,128)(2,1)S(1)}, bf16[2,256,256]{2,1,0:T(8,128)(2,1)S(1)}, u32[]{:S(2)}, u32[]{:S(2)}) collective-permute-start(bf16[2,256,256]{2,1,0:T(8,128)(2,1)S(1)} %pad_maximum_fusion.40), channel_id=1, source_target_pairs={{0,1},{1,0},{2,3},{3,2},{4,5},{5,4},{6,7},{7,6},{8,9},{9,8},{10,11... | collective-permute-start | bytes 786440 | tf_op jit(solution)/shard_map/ppermute | solution.py:11
  18.2 3.8 %collective-permute-start.3 = (bf16[2,256,256]{2,1,0:T(8,128)(2,1)S(1)}, bf16[2,256,256]{2,1,0:T(8,128)(2,1)S(1)}, u32[]{:S(2)}, u32[]{:S(2)}) collective-permute-start(bf16[2,256,256]{2,1,0:T(8,128)(2,1)S(1)} %get-tuple-element.678), channel_id=1, source_target_pairs={{0,1},{1,0},{2,3},{3,2},{4,5},{5,4},{6,7},{7,6},{8,9},{9,8},{10,11... | collective-permute-start | bytes 786440 | tf_op jit(solution)/shard_map/ppermute | solution.py:11
  18.3 9.3 %collective-permute-start.2 = (bf16[2,256,256]{2,1,0:T(8,128)(2,1)S(1)}, bf16[2,256,256]{2,1,0:T(8,128)(2,1)}, u32[]{:S(2)}, u32[]{:S(2)}) collective-permute-start(bf16[2,256,256]{2,1,0:T(8,128)(2,1)S(1)} %pad_maximum_fusion.40), channel_id=1, source_target_pairs={{0,2},{1,3},{2,0},{3,1},{4,6},{5,7},{6,4},{7,5},{8,10},{9,11},{10,... | collective-permute-start | bytes 786440 | tf_op jit(solution)/shard_map/ppermute | solution.py:11
  20.1 13.0 %collective-permute-start.5 = (bf16[2,256,256]{2,1,0:T(8,128)(2,1)S(1)}, bf16[2,256,256]{2,1,0:T(8,128)(2,1)S(1)}, u32[]{:S(2)}, u32[]{:S(2)}) collective-permute-start(bf16[2,256,256]{2,1,0:T(8,128)(2,1)S(1)} %get-tuple-element.673), channel_id=1, source_target_pairs={{0,2},{1,3},{2,0},{3,1},{4,6},{5,7},{6,4},{7,5},{8,10},{9,11},{10,... | collective-permute-start | bytes 786440 | tf_op jit(solution)/shard_map/ppermute | solution.py:11
  22.0 5.7 %collective-permute-start.8 = (bf16[2,256,256]{2,1,0:T(8,128)(2,1)S(1)}, bf16[2,256,256]{2,1,0:T(8,128)(2,1)S(1)}, u32[]{:S(2)}, u32[]{:S(2)}) collective-permute-start(bf16[2,256,256]{2,1,0:T(8,128)(2,1)S(1)} %get-tuple-element.682), channel_id=1, source_target_pairs={{0,1},{1,0},{2,3},{3,2},{4,5},{5,4},{6,7},{7,6},{8,9},{9,8},{10,11... | collective-permute-start | bytes 786440 | tf_op jit(solution)/shard_map/ppermute | solution.py:11
  23.7 9.5 %collective-permute-start.6 = (bf16[2,256,256]{2,1,0:T(8,128)(2,1)S(1)}, bf16[2,256,256]{2,1,0:T(8,128)(2,1)S(1)}, u32[]{:S(2)}, u32[]{:S(2)}) collective-permute-start(bf16[2,256,256]{2,1,0:T(8,128)(2,1)S(1)} %get-tuple-element.680), channel_id=1, source_target_pairs={{0,1},{1,0},{2,3},{3,2},{4,5},{5,4},{6,7},{7,6},{8,9},{9,8},{10,11... | collective-permute-start | bytes 786440 | tf_op jit(solution)/shard_map/ppermute | solution.py:11
  24.2 14.6 %collective-permute-start.11 = (bf16[2,256,256]{2,1,0:T(8,128)(2,1)S(1)}, bf16[2,256,256]{2,1,0:T(8,128)(2,1)}, u32[]{:S(2)}, u32[]{:S(2)}) collective-permute-start(bf16[2,256,256]{2,1,0:T(8,128)(2,1)S(1)} %get-tuple-element.680), channel_id=1, source_target_pairs={{0,2},{1,3},{2,0},{3,1},{4,6},{5,7},{6,4},{7,5},{8,10},{9,11},{10,... | collective-permute-start | bytes 786440 | tf_op jit(solution)/shard_map/ppermute | solution.py:11
  32.8 4.3 %collective-permute-start.14 = (bf16[2,256,256]{2,1,0:T(8,128)(2,1)S(1)}, bf16[2,256,256]{2,1,0:T(8,128)(2,1)S(1)}, u32[]{:S(2)}, u32[]{:S(2)}) collective-permute-start(bf16[2,256,256]{2,1,0:T(8,128)(2,1)S(1)} %get-tuple-element.683), channel_id=1, source_target_pairs={{0,1},{1,0},{2,3},{3,2},{4,5},{5,4},{6,7},{7,6},{8,9},{9,8},{10,11... | collective-permute-start | bytes 786440 | tf_op jit(solution)/shard_map/ppermute | solution.py:11
  34.7 4.1 %collective-permute-start.10 = (bf16[2,256,256]{2,1,0:T(8,128)(2,1)S(1)}, bf16[2,256,256]{2,1,0:T(8,128)(2,1)S(1)}, u32[]{:S(2)}, u32[]{:S(2)}) collective-permute-start(bf16[2,256,256]{2,1,0:T(8,128)(2,1)S(1)} %get-tuple-element.681), channel_id=1, source_target_pairs={{0,1},{1,0},{2,3},{3,2},{4,5},{5,4},{6,7},{7,6},{8,9},{9,8},{10,11... | collective-permute-start | bytes 786440 | tf_op jit(solution)/shard_map/ppermute | solution.py:11
  35.1 20.2 %collective-permute-start.12 = (bf16[2,256,256]{2,1,0:T(8,128)(2,1)S(1)}, bf16[2,256,256]{2,1,0:T(8,128)(2,1)S(1)}, u32[]{:S(2)}, u32[]{:S(2)}) collective-permute-start(bf16[2,256,256]{2,1,0:T(8,128)(2,1)S(1)} %get-tuple-element.675), channel_id=1, source_target_pairs={{0,2},{1,3},{2,0},{3,1},{4,6},{5,7},{6,4},{7,5},{8,10},{9,11},{10,... | collective-permute-start | bytes 786440 | tf_op jit(solution)/shard_map/ppermute | solution.py:11
  36.8 13.1 %collective-permute-start.9 = (bf16[2,256,256]{2,1,0:T(8,128)(2,1)S(1)}, bf16[2,256,256]{2,1,0:T(8,128)(2,1)}, u32[]{:S(2)}, u32[]{:S(2)}) collective-permute-start(bf16[2,256,256]{2,1,0:T(8,128)(2,1)S(1)} %get-tuple-element.683), channel_id=1, source_target_pairs={{0,2},{1,3},{2,0},{3,1},{4,6},{5,7},{6,4},{7,5},{8,10},{9,11},{10,... | collective-permute-start | bytes 786440 | tf_op jit(solution)/shard_map/ppermute | solution.py:11
  38.7 11.3 %collective-permute-start.15 = (bf16[2,256,256]{2,1,0:T(8,128)(2,1)S(1)}, bf16[2,256,256]{2,1,0:T(8,128)(2,1)S(1)}, u32[]{:S(2)}, u32[]{:S(2)}) collective-permute-start(bf16[2,256,256]{2,1,0:T(8,128)(2,1)S(1)} %get-tuple-element.687), channel_id=1, source_target_pairs={{0,1},{1,0},{2,3},{3,2},{4,5},{5,4},{6,7},{7,6},{8,9},{9,8},{10,11... | collective-permute-start | bytes 786440 | tf_op jit(solution)/shard_map/ppermute | solution.py:11
  44.0 11.3 %collective-permute-start.13 = (bf16[2,256,256]{2,1,0:T(8,128)(2,1)S(1)}, bf16[2,256,256]{2,1,0:T(8,128)(2,1)}, u32[]{:S(2)}, u32[]{:S(2)}) collective-permute-start(bf16[2,256,256]{2,1,0:T(8,128)(2,1)S(1)} %get-tuple-element.685), channel_id=1, source_target_pairs={{0,1},{1,0},{2,3},{3,2},{4,5},{5,4},{6,7},{7,6},{8,9},{9,8},{10,11... | collective-permute-start | bytes 786440 | tf_op jit(solution)/shard_map/ppermute | solution.py:11
  44.5 29.3 %collective-permute-start.18 = (bf16[2,256,256]{2,1,0:T(8,128)(2,1)S(1)}, bf16[2,256,256]{2,1,0:T(8,128)(2,1)}, u32[]{:S(2)}, u32[]{:S(2)}) collective-permute-start(bf16[2,256,256]{2,1,0:T(8,128)(2,1)S(1)} %get-tuple-element.685), channel_id=1, source_target_pairs={{0,2},{1,3},{2,0},{3,1},{4,6},{5,7},{6,4},{7,5},{8,10},{9,11},{10,... | collective-permute-start | bytes 786440 | tf_op jit(solution)/shard_map/ppermute | solution.py:11
  55.2 12.8 %collective-permute-start.21 = (bf16[2,256,256]{2,1,0:T(8,128)(2,1)S(1)}, bf16[2,256,256]{2,1,0:T(8,128)(2,1)}, u32[]{:S(2)}, u32[]{:S(2)}) collective-permute-start(bf16[2,256,256]{2,1,0:T(8,128)(2,1)S(1)} %get-tuple-element.688), channel_id=1, source_target_pairs={{0,1},{1,0},{2,3},{3,2},{4,5},{5,4},{6,7},{7,6},{8,9},{9,8},{10,11... | collective-permute-start | bytes 786440 | tf_op jit(solution)/shard_map/ppermute | solution.py:11
  60.7 13.2 %collective-permute-start.17 = (bf16[2,256,256]{2,1,0:T(8,128)(2,1)S(1)}, bf16[2,256,256]{2,1,0:T(8,128)(2,1)}, u32[]{:S(2)}, u32[]{:S(2)}) collective-permute-start(bf16[2,256,256]{2,1,0:T(8,128)(2,1)S(1)} %get-tuple-element.686), channel_id=1, source_target_pairs={{0,1},{1,0},{2,3},{3,2},{4,5},{5,4},{6,7},{7,6},{8,9},{9,8},{10,11... | collective-permute-start | bytes 786440 | tf_op jit(solution)/shard_map/ppermute | solution.py:11
  61.2 34.4 %collective-permute-start.19 = (bf16[2,256,256]{2,1,0:T(8,128)(2,1)S(1)}, bf16[2,256,256]{2,1,0:T(8,128)(2,1)S(1)}, u32[]{:S(2)}, u32[]{:S(2)}) collective-permute-start(bf16[2,256,256]{2,1,0:T(8,128)(2,1)S(1)} %get-tuple-element.672), channel_id=1, source_target_pairs={{0,2},{1,3},{2,0},{3,1},{4,6},{5,7},{6,4},{7,5},{8,10},{9,11},{10,... | collective-permute-start | bytes 786440 | tf_op jit(solution)/shard_map/ppermute | solution.py:11
  64.9 0.7 copy-start.4
  67.5 17.3 %collective-permute-start.16 = (bf16[2,256,256]{2,1,0:T(8,128)(2,1)S(1)}, bf16[2,256,256]{2,1,0:T(8,128)(2,1)}, u32[]{:S(2)}, u32[]{:S(2)}) collective-permute-start(bf16[2,256,256]{2,1,0:T(8,128)(2,1)S(1)} %get-tuple-element.688), channel_id=1, source_target_pairs={{0,2},{1,3},{2,0},{3,1},{4,6},{5,7},{6,4},{7,5},{8,10},{9,11},{10,... | collective-permute-start | bytes 786440 | tf_op jit(solution)/shard_map/ppermute | solution.py:11
  73.9 11.0 %collective-permute-start.22 = (bf16[2,256,256]{2,1,0:T(8,128)(2,1)}, bf16[2,256,256]{2,1,0:T(8,128)(2,1)}, u32[]{:S(2)}, u32[]{:S(2)}) collective-permute-start(bf16[2,256,256]{2,1,0:T(8,128)(2,1)} %get-tuple-element.692), channel_id=1, source_target_pairs={{0,1},{1,0},{2,3},{3,2},{4,5},{5,4},{6,7},{7,6},{8,9},{9,8},{10,11... | collective-permute-start | bytes 786440 | tf_op jit(solution)/shard_map/ppermute | solution.py:11
  79.3 16.3 %collective-permute-start.20 = (bf16[2,256,256]{2,1,0:T(8,128)(2,1)S(1)}, bf16[2,256,256]{2,1,0:T(8,128)(2,1)S(1)}, u32[]{:S(2)}, u32[]{:S(2)}) collective-permute-start(bf16[2,256,256]{2,1,0:T(8,128)(2,1)S(1)} %get-tuple-element.690), channel_id=1, source_target_pairs={{0,1},{1,0},{2,3},{3,2},{4,5},{5,4},{6,7},{7,6},{8,9},{9,8},{10,11... | collective-permute-start | bytes 786440 | tf_op jit(solution)/shard_map/ppermute | solution.py:11
  83.3 1.6 copy-start.5
  94.0 21.8 %collective-permute-start.26 = (bf16[2,256,256]{2,1,0:T(8,128)(2,1)S(1)}, bf16[2,256,256]{2,1,0:T(8,128)(2,1)}, u32[]{:S(2)}, u32[]{:S(2)}) collective-permute-start(bf16[2,256,256]{2,1,0:T(8,128)(2,1)S(1)} %get-tuple-element.693), channel_id=1, source_target_pairs={{0,1},{1,0},{2,3},{3,2},{4,5},{5,4},{6,7},{7,6},{8,9},{9,8},{10,11... | collective-permute-start | bytes 786440 | tf_op jit(solution)/shard_map/ppermute | solution.py:11
  94.1 30.4 %collective-permute-start.23 = (bf16[2,256,256]{2,1,0:T(8,128)(2,1)S(1)}, bf16[2,256,256]{2,1,0:T(8,128)(2,1)}, u32[]{:S(2)}, u32[]{:S(2)}) collective-permute-start(bf16[2,256,256]{2,1,0:T(8,128)(2,1)S(1)} %get-tuple-element.693), channel_id=1, source_target_pairs={{0,2},{1,3},{2,0},{3,1},{4,6},{5,7},{6,4},{7,5},{8,10},{9,11},{10,... | collective-permute-start | bytes 786440 | tf_op jit(solution)/shard_map/ppermute | solution.py:11
  97.2 27.3 %collective-permute-start.24 = (bf16[2,256,256]{2,1,0:T(8,128)(2,1)S(1)}, bf16[2,256,256]{2,1,0:T(8,128)(2,1)}, u32[]{:S(2)}, u32[]{:S(2)}) collective-permute-start(bf16[2,256,256]{2,1,0:T(8,128)(2,1)S(1)} %get-tuple-element.691), channel_id=1, source_target_pairs={{0,1},{1,0},{2,3},{3,2},{4,5},{5,4},{6,7},{7,6},{8,9},{9,8},{10,11... | collective-permute-start | bytes 786440 | tf_op jit(solution)/shard_map/ppermute | solution.py:11
  108.8 31.8 %collective-permute-start.25 = (bf16[2,256,256]{2,1,0:T(8,128)(2,1)S(1)}, bf16[2,256,256]{2,1,0:T(8,128)(2,1)S(1)}, u32[]{:S(2)}, u32[]{:S(2)}) collective-permute-start(bf16[2,256,256]{2,1,0:T(8,128)(2,1)S(1)} %get-tuple-element.690), channel_id=1, source_target_pairs={{0,2},{1,3},{2,0},{3,1},{4,6},{5,7},{6,4},{7,5},{8,10},{9,11},{10,... | collective-permute-start | bytes 786440 | tf_op jit(solution)/shard_map/ppermute | solution.py:11
  121.0 24.9 %collective-permute-start.27 = (bf16[2,256,256]{2,1,0:T(8,128)(2,1)S(1)}, bf16[2,256,256]{2,1,0:T(8,128)(2,1)S(1)}, u32[]{:S(2)}, u32[]{:S(2)}) collective-permute-start(bf16[2,256,256]{2,1,0:T(8,128)(2,1)S(1)} %get-tuple-element.696), channel_id=1, source_target_pairs={{0,1},{1,0},{2,3},{3,2},{4,5},{5,4},{6,7},{7,6},{8,9},{9,8},{10,11... | collective-permute-start | bytes 786440 | tf_op jit(solution)/shard_map/ppermute | solution.py:11
  124.5 6.5 %copy-start.1 = (f32[2,256,256]{2,1,0:T(8,128)S(1)}, f32[2,256,256]{2,1,0:T(8,128)}, u32[]{:S(2)}) copy-start(f32[2,256,256]{2,1,0:T(8,128)} %get-tuple-element.689) | copy-start | bytes 1572868
  133.7 18.0 %all-to-all-start = ((bf16[8,1,2,16,256]{4,3,2,1,0:T(8,128)(2,1)}), bf16[8,1,2,16,256]{4,3,2,1,0:T(8,128)(2,1)S(1)}, u32[]{:S(2)}, u32[]{:S(2)}) async-start(bf16[8,1,2,16,256]{4,3,2,1,0:T(8,128)(2,1)} %copy.23), calls=%async_computation | async-start | bytes 262144 | tf_op jit(solution)/shard_map/all_to_all | solution.py:107
  145.8 0.7 copy-start.2
  151.7 0.7 copy-start.3
where the time goes:
time: 176 us; the launch traced here: 175 us
  matrix products  88.4 us (50%)
  starting transfers between devices  32.4 us (18%)
  blocking collectives  19.3 us (11%)
  waiting for transfers between devices  14.4 us (8%)
  local copies, waits for them, and re-layouts  11.5 us (7%)
  other arithmetic  5.75 us (3%)
    dot_general x160, matrix products, single(): return jnp.dot(leading, trailing, preferred_element_type=jnp.float32)  85 us
    ppermute x28, starting transfers between devices, partner(): lax.ppermute(shard, axis, [(i, i ^ 1 << stride) for i in range(lax.axis_s...  25.5 us
    psum x1, blocking collectives, local(): lax.psum(weighted.astype(jnp.bfloat16), 'energy').astype(jnp.float32)  19.3 us
    ppermute x28, waiting for transfers between devices, partner(): lax.ppermute(shard, axis, [(i, i ^ 1 << stride) for i in range(lax.axis_s...  14.4 us
    all_to_all x1, starting transfers between devices, local(): lax.all_to_all(partial_terms[:, None].astype(jnp.bfloat16), 'rows', split...  6.89 us
    unnamed x17, local copies, waits for them, and re-layouts  4.34 us
  transfers between devices with their start and end apart: 29, of which 4 were waited for; matrix products, arithmetic and copies ran while one was open for 57% of the time, Pallas kernels for 0%

commit v1 on v0

--- a/solution.py
+++ b/solution.py
@@ -118,7 +118,9 @@
     )
     injection = jnp.take(slots, source_slot, axis=0)
     weighted = jnp.tensordot(weights, injection, axes=1, precision=lax.Precision.HIGHEST)
-    integrated = lax.psum(weighted.astype(jnp.bfloat16), "energy").astype(jnp.float32)
+    integrated = jnp.sum(lax.all_gather(weighted.astype(jnp.bfloat16), "energy"), axis=0).astype(
+        jnp.float32
+    )
     return (injection, integrated, forward[None], backward[None])
 
 

time: 176 us -> 171 us (0.972)
  blocking collectives: 19.3 us -> 13.6 us
    psum x1 -> x0, blocking collectives: 19.3 us -> none  [local(): lax.psum(weighted.astype(jnp.bfloat16), 'energy').astype(jnp.float32)]
    all_gather x0 -> x1, blocking collectives: none -> 13.6 us  [local(): lax.all_gather(weighted.astype(jnp.bfloat16), 'energy')]
  transfers between devices with their start and end apart: 29 -> 29, of which waited for: 4 -> 4; matrix products, arithmetic and copies ran while one was open for 57% -> 59% of each run, Pallas kernels for 0% -> 0%
where the time goes in v1:
time: 171 us; the launch traced here: 169 us
  matrix products  88.4 us (52%)
  starting transfers between devices  32.4 us (19%)
  waiting for transfers between devices  14.4 us (8%)
  blocking collectives  13.6 us (8%)
  local copies, waits for them, and re-layouts  11.5 us (7%)
  other arithmetic  5.77 us (3%)
  loops' own time  1.74 us (1%)
    dot_general x160, matrix products, single(): return jnp.dot(leading, trailing, preferred_element_type=jnp.float32)  85 us
    ppermute x28, starting transfers between devices, partner(): lax.ppermute(shard, axis, [(i, i ^ 1 << stride) for i in range(lax.axis_s...  25.5 us
    ppermute x28, waiting for transfers between devices, partner(): lax.ppermute(shard, axis, [(i, i ^ 1 << stride) for i in range(lax.axis_s...  14.4 us
    all_gather x1, blocking collectives, local(): lax.all_gather(weighted.astype(jnp.bfloat16), 'energy')  13.6 us
    all_to_all x1, starting transfers between devices, local(): lax.all_to_all(partial_terms[:, None].astype(jnp.bfloat16), 'rows', split...  6.89 us
    unnamed x17, local copies, waits for them, and re-layouts  4.34 us
  transfers between devices with their start and end apart: 29, of which 4 were waited for; matrix products, arithmetic and copies ran while one was open for 59% of the time, Pallas kernels for 0%

profile of v1, /device:TPU:0, one launch (start us, length us, event | category | flops | bytes accessed | tf_op | source)
XLA Modules:
  0.0 169.0 jit_solution(16597010704612505021)
XLA Ops:
  1.7 3.0 %collective-permute-start.4 = (bf16[2,256,256]{2,1,0:T(8,128)(2,1)S(1)}, bf16[2,256,256]{2,1,0:T(8,128)(2,1)S(1)}, u32[]{:S(2)}, u32[]{:S(2)}) collective-permute-start(bf16[2,256,256]{2,1,0:T(8,128)(2,1)S(1)} %constant_dynamic-slice_fusion.1), channel_id=1, source_target_pairs={{0,2},{1,3},{2,0},{3,1},{4,6},{5,7},{6,4},{7,5},{8,10},{9,11},{10,... | collective-permute-start | bytes 786440 | tf_op jit(solution)/shard_map/ppermute | solution.py:11
  4.7 1.3 slice_bitcast_fusion
  7.9 8.7 %collective-permute-done = bf16[2,256,256]{2,1,0:T(8,128)(2,1)S(1)} collective-permute-done((bf16[2,256,256]{2,1,0:T(8,128)(2,1)S(1)}, bf16[2,256,256]{2,1,0:T(8,128)(2,1)S(1)}, u32[]{:S(2)}, u32[]{:S(2)}) %collective-permute-start) | collective-permute-done | bytes 262176 | tf_op jit(solution)/shard_map/ppermute | solution.py:11
  16.6 1.6 conditional.100
  18.3 1.8 %collective-permute-start.2 = (bf16[2,256,256]{2,1,0:T(8,128)(2,1)S(1)}, bf16[2,256,256]{2,1,0:T(8,128)(2,1)}, u32[]{:S(2)}, u32[]{:S(2)}) collective-permute-start(bf16[2,256,256]{2,1,0:T(8,128)(2,1)S(1)} %pad_maximum_fusion.40), channel_id=1, source_target_pairs={{0,2},{1,3},{2,0},{3,1},{4,6},{5,7},{6,4},{7,5},{8,10},{9,11},{10,... | collective-permute-start | bytes 786440 | tf_op jit(solution)/shard_map/ppermute | solution.py:11
  20.4 1.6 conditional.104
  22.1 1.6 conditional.102
  24.2 1.8 %collective-permute-start.11 = (bf16[2,256,256]{2,1,0:T(8,128)(2,1)S(1)}, bf16[2,256,256]{2,1,0:T(8,128)(2,1)}, u32[]{:S(2)}, u32[]{:S(2)}) collective-permute-start(bf16[2,256,256]{2,1,0:T(8,128)(2,1)S(1)} %get-tuple-element.680), channel_id=1, source_target_pairs={{0,2},{1,3},{2,0},{3,1},{4,6},{5,7},{6,4},{7,5},{8,10},{9,11},{10,... | collective-permute-start | bytes 786440 | tf_op jit(solution)/shard_map/ppermute | solution.py:11
  26.0 1.7 collective-permute-done.2
  27.6 5.2 %conditional.105 = (bf16[2,256,256]{2,1,0:T(8,128)(2,1)S(1)}) conditional(s32[]{:T(128)} %convert_element_type.234, (bf16[2,256,256]{2,1,0:T(8,128)(2,1)S(1)}, bf16[2,256,256]{2,1,0:T(8,128)(2,1)}, bf16[2,256,256]{2,1,0:T(8,128)(2,1)S(1)}, bf16[256,256]{1,0:T(8,128)(2,1)S(1)}, bf16[256,256]{1,0:T(8,128)(2,1)S(1)}) %tuple.379, ...), branch_computations={%region_11.12_spmd, %region_12.13_spmd} | conditional | flops 269090816 | bytes 6029320
  33.1 1.6 conditional.103
  35.1 1.8 %collective-permute-start.12 = (bf16[2,256,256]{2,1,0:T(8,128)(2,1)S(1)}, bf16[2,256,256]{2,1,0:T(8,128)(2,1)S(1)}, u32[]{:S(2)}, u32[]{:S(2)}) collective-permute-start(bf16[2,256,256]{2,1,0:T(8,128)(2,1)S(1)} %get-tuple-element.675), channel_id=1, source_target_pairs={{0,2},{1,3},{2,0},{3,1},{4,6},{5,7},{6,4},{7,5},{8,10},{9,11},{10,... | collective-permute-start | bytes 786440 | tf_op jit(solution)/shard_map/ppermute | solution.py:11
  37.1 1.6 conditional.109
  38.8 5.2 %conditional.107 = (bf16[2,256,256]{2,1,0:T(8,128)(2,1)S(1)}) conditional(s32[]{:T(128)} %convert_element_type.234, (bf16[2,256,256]{2,1,0:T(8,128)(2,1)S(1)}, bf16[2,256,256]{2,1,0:T(8,128)(2,1)}, bf16[2,256,256]{2,1,0:T(8,128)(2,1)S(1)}, bf16[2,256,256]{2,1,0:T(8,128)(2,1)S(1)}) %tuple.302, (bf16[2,256,256]{2,1,0:T(8,128)(2,1)S(1)}, ...), branch_computations={%region_15.16_spmd, %region_16.17_spmd} | conditional | flops 269090816 | bytes 6029320
  44.5 1.8 %collective-permute-start.18 = (bf16[2,256,256]{2,1,0:T(8,128)(2,1)S(1)}, bf16[2,256,256]{2,1,0:T(8,128)(2,1)}, u32[]{:S(2)}, u32[]{:S(2)}) collective-permute-start(bf16[2,256,256]{2,1,0:T(8,128)(2,1)S(1)} %get-tuple-element.685), channel_id=1, source_target_pairs={{0,2},{1,3},{2,0},{3,1},{4,6},{5,7},{6,4},{7,5},{8,10},{9,11},{10,... | collective-permute-start | bytes 786440 | tf_op jit(solution)/shard_map/ppermute | solution.py:11
  46.3 3.7 %collective-permute-done.9 = bf16[2,256,256]{2,1,0:T(8,128)(2,1)} collective-permute-done((bf16[2,256,256]{2,1,0:T(8,128)(2,1)S(1)}, bf16[2,256,256]{2,1,0:T(8,128)(2,1)}, u32[]{:S(2)}, u32[]{:S(2)}) %collective-permute-start.9) | collective-permute-done | bytes 262176 | tf_op jit(solution)/shard_map/ppermute | solution.py:11
  50.0 5.2 %conditional.110 = (bf16[2,256,256]{2,1,0:T(8,128)(2,1)S(1)}) conditional(s32[]{:T(128)} %convert_element_type.234, (bf16[2,256,256]{2,1,0:T(8,128)(2,1)S(1)}, bf16[2,256,256]{2,1,0:T(8,128)(2,1)}, bf16[2,256,256]{2,1,0:T(8,128)(2,1)S(1)}, bf16[2,256,256]{2,1,0:T(8,128)(2,1)S(1)}) %tuple.308, (bf16[2,256,256]{2,1,0:T(8,128)(2,1)S(1)}, ...), branch_computations={%region_21.22_spmd, %region_22.23_spmd} | conditional | flops 269090816 | bytes 6029320
  55.3 5.4 %conditional.108 = (bf16[2,256,256]{2,1,0:T(8,128)(2,1)S(1)}) conditional(s32[]{:T(128)} %convert_element_type.234, (bf16[2,256,256]{2,1,0:T(8,128)(2,1)S(1)}, bf16[2,256,256]{2,1,0:T(8,128)(2,1)S(1)}, bf16[2,256,256]{2,1,0:T(8,128)(2,1)}, bf16[2,256,256]{2,1,0:T(8,128)(2,1)S(1)}) %tuple.304, (bf16[2,256,256]{2,1,0:T(8,128)(2,1)S(1)}, ...), branch_computations={%region_17.18_spmd, %region_18.19_spmd} | conditional | flops 269090816 | bytes 6029320
  61.2 1.6 collective-permute-start.19
  65.6 2.0 %convolution_convert_fusion = bf16[8,16384]{1,0:T(8,128)(2,1)} fusion(bf16[12,16384]{1,0:T(8,128)(2,1)} %bitcast.1813, s32[12]{0:T(128)S(1)} %copy-done.4), kind=kOutput, calls=%fused_computation.1673 | convolution fusion | flops 3276896 | bytes 655408 | tf_op jit(solution)/shard_map/dot_general | solution.py:91
  68.0 5.9 %conditional.114 = (bf16[2,256,256]{2,1,0:T(8,128)(2,1)}) conditional(s32[]{:T(128)} %convert_element_type.234, (bf16[2,256,256]{2,1,0:T(8,128)(2,1)S(1)}, bf16[2,256,256]{2,1,0:T(8,128)(2,1)S(1)}, bf16[2,256,256]{2,1,0:T(8,128)(2,1)}, bf16[2,256,256]{2,1,0:T(8,128)(2,1)S(1)}) %tuple.316, (bf16[2,256,256]{2,1,0:T(8,128)(2,1)S(1)}, ...), branch_computations={%region_29.30_spmd, %region_30.31_spmd} | conditional | flops 269090816 | bytes 6029320
  73.9 5.5 %conditional.112 = (bf16[2,256,256]{2,1,0:T(8,128)(2,1)S(1)}) conditional(s32[]{:T(128)} %convert_element_type.234, (bf16[2,256,256]{2,1,0:T(8,128)(2,1)S(1)}, bf16[2,256,256]{2,1,0:T(8,128)(2,1)}, bf16[2,256,256]{2,1,0:T(8,128)(2,1)}, bf16[2,256,256]{2,1,0:T(8,128)(2,1)S(1)}) %tuple.312, (bf16[2,256,256]{2,1,0:T(8,128)(2,1)S(1)}, ...), branch_computations={%region_25.26_spmd, %region_26.27_spmd} | conditional | flops 269090816 | bytes 6029320
  75.4 1.2 fusion.852
  79.3 3.9 %collective-permute-start.20 = (bf16[2,256,256]{2,1,0:T(8,128)(2,1)S(1)}, bf16[2,256,256]{2,1,0:T(8,128)(2,1)S(1)}, u32[]{:S(2)}, u32[]{:S(2)}) collective-permute-start(bf16[2,256,256]{2,1,0:T(8,128)(2,1)S(1)} %get-tuple-element.690), channel_id=1, source_target_pairs={{0,1},{1,0},{2,3},{3,2},{4,5},{5,4},{6,7},{7,6},{8,9},{9,8},{10,11... | collective-permute-start | bytes 786440 | tf_op jit(solution)/shard_map/ppermute | solution.py:11
  83.3 1.6 constant_dynamic-slice_fusion.2
  84.9 9.1 %conditional.115 = (bf16[2,256,256]{2,1,0:T(8,128)(2,1)S(1)}) conditional(s32[]{:T(128)} %convert_element_type.234, (bf16[2,256,256]{2,1,0:T(8,128)(2,1)}, bf16[2,256,256]{2,1,0:T(8,128)(2,1)}, bf16[2,256,256]{2,1,0:T(8,128)(2,1)}, bf16[2,256,256]{2,1,0:T(8,128)(2,1)S(1)}) %tuple.318, (bf16[2,256,256]{2,1,0:T(8,128)(2,1)}, ...), branch_computations={%region_31.32_spmd, %region_32.33_spmd} | conditional | flops 269090816 | bytes 6029320
  87.1 1.2 convolution_add_fusion.125
  88.3 1.2 fusion.1068
  91.6 1.2 convolution_add_fusion.127
  94.1 1.6 collective-permute-start.23
  95.6 1.6 conditional.113
  98.4 5.2 %conditional.101 = (f32[2,256,256]{2,1,0:T(8,128)S(1)}) conditional(s32[]{:T(128)} %convert_element_type.234, (bf16[2,256,256]{2,1,0:T(8,128)(2,1)S(1)}, bf16[2,256,256]{2,1,0:T(8,128)(2,1)}, bf16[2,256,256]{2,1,0:T(8,128)(2,1)S(1)}, bf16[256,256]{1,0:T(8,128)(2,1)S(1)}, bf16[256,256]{1,0:T(8,128)(2,1)S(1)}) %tuple.381, ...), branch_computations={%region_3.4_spmd, %region_4.5_spmd} | conditional | flops 268959744 | bytes 6815752 | solution.py:42
  103.6 5.2 %conditional.106 = (f32[2,256,256]{2,1,0:T(8,128)S(1)}) conditional(s32[]{:T(128)} %convert_element_type.234, (bf16[2,256,256]{2,1,0:T(8,128)(2,1)S(1)}, bf16[2,256,256]{2,1,0:T(8,128)(2,1)}, bf16[2,256,256]{2,1,0:T(8,128)(2,1)S(1)}, bf16[2,256,256]{2,1,0:T(8,128)(2,1)S(1)}) %tuple.300, (bf16[2,256,256]{2,1,0:T(8,128)(2,1)S(1)}, ...), branch_computations={%region_13.14_spmd, %region_14.15_spmd} | conditional | flops 268959744 | bytes 6815752 | solution.py:42
  109.5 6.3 %conditional.111 = (f32[2,256,256]{2,1,0:T(8,128)}) conditional(s32[]{:T(128)} %convert_element_type.234, (bf16[2,256,256]{2,1,0:T(8,128)(2,1)S(1)}, bf16[2,256,256]{2,1,0:T(8,128)(2,1)}, bf16[2,256,256]{2,1,0:T(8,128)(2,1)}, bf16[2,256,256]{2,1,0:T(8,128)(2,1)S(1)}) %tuple.310, (bf16[2,256,256]{2,1,0:T(8,128)(2,1)S(1)}, ...), branch_computations={%region_23.24_spmd, %region_24.25_spmd} | conditional | flops 268959744 | bytes 6815752 | solution.py:42
  109.9 1.2 convolution_add_fusion.93
  111.1 1.2 fusion.780
  112.6 1.2 convolution_add_fusion.95
  113.8 1.2 fusion.781
  115.8 5.2 %conditional.118 = (bf16[2,256,256]{2,1,0:T(8,128)(2,1)S(1)}) conditional(s32[]{:T(128)} %convert_element_type.234, (bf16[2,256,256]{2,1,0:T(8,128)(2,1)S(1)}, bf16[2,256,256]{2,1,0:T(8,128)(2,1)S(1)}, bf16[2,256,256]{2,1,0:T(8,128)(2,1)}, bf16[2,256,256]{2,1,0:T(8,128)(2,1)S(1)}) %tuple.324, (bf16[2,256,256]{2,1,0:T(8,128)(2,1)S(1)}, ...), branch_computations={%region_39.40_spmd, %region_40.41_spmd} | conditional | flops 269090816 | bytes 6029320
  121.0 3.5 %collective-permute-start.27 = (bf16[2,256,256]{2,1,0:T(8,128)(2,1)S(1)}, bf16[2,256,256]{2,1,0:T(8,128)(2,1)S(1)}, u32[]{:S(2)}, u32[]{:S(2)}) collective-permute-start(bf16[2,256,256]{2,1,0:T(8,128)(2,1)S(1)} %get-tuple-element.696), channel_id=1, source_target_pairs={{0,1},{1,0},{2,3},{3,2},{4,5},{5,4},{6,7},{7,6},{8,9},{9,8},{10,11... | collective-permute-start | bytes 786440 | tf_op jit(solution)/shard_map/ppermute | solution.py:11
  124.5 6.5 %conditional.116 = (f32[2,256,256]{2,1,0:T(8,128)}) conditional(s32[]{:T(128)} %convert_element_type.234, (bf16[2,256,256]{2,1,0:T(8,128)(2,1)S(1)}, bf16[2,256,256]{2,1,0:T(8,128)(2,1)}, bf16[2,256,256]{2,1,0:T(8,128)(2,1)}, bf16[2,256,256]{2,1,0:T(8,128)(2,1)S(1)}) %tuple.320, (bf16[2,256,256]{2,1,0:T(8,128)(2,1)S(1)}, ...), branch_computations={%region_33.34_spmd, %region_34.35_spmd} | conditional | flops 268959744 | bytes 6815752 | solution.py:42
  126.3 1.2 fusion.1140
  127.9 1.2 convolution_add_fusion.135
  131.0 1.2 add_convert_fusion
  133.7 6.9 %all-to-all-start = ((bf16[8,1,2,16,256]{4,3,2,1,0:T(8,128)(2,1)}), bf16[8,1,2,16,256]{4,3,2,1,0:T(8,128)(2,1)S(1)}, u32[]{:S(2)}, u32[]{:S(2)}) async-start(bf16[8,1,2,16,256]{4,3,2,1,0:T(8,128)(2,1)} %copy.23), calls=%async_computation | async-start | bytes 262144 | tf_op jit(solution)/shard_map/all_to_all | solution.py:107
  140.6 5.2 %conditional.117 = (bf16[1,2,256,256]{3,2,1,0:T(8,128)(2,1)S(1)}) conditional(s32[]{:T(128)} %convert_element_type.234, (bf16[2,256,256]{2,1,0:T(8,128)(2,1)S(1)}, bf16[2,256,256]{2,1,0:T(8,128)(2,1)S(1)}, bf16[2,256,256]{2,1,0:T(8,128)(2,1)}, bf16[2,256,256]{2,1,0:T(8,128)(2,1)S(1)}) %tuple.322, (bf16[2,256,256]{2,1,0:T(8,128)(2,1)S(1)}, ...), branch_computations={%region_37.38_spmd, %region_38.39_spmd} | conditional | flops 269090816 | bytes 6029320
  146.5 5.2 %conditional.119 = (bf16[1,2,256,256]{3,2,1,0:T(8,128)(2,1)S(1)}) conditional(s32[]{:T(128)} %convert_element_type.234, (bf16[2,256,256]{2,1,0:T(8,128)(2,1)S(1)}, bf16[2,256,256]{2,1,0:T(8,128)(2,1)}, bf16[2,256,256]{2,1,0:T(8,128)(2,1)S(1)}, bf16[2,256,256]{2,1,0:T(8,128)(2,1)S(1)}) %tuple.326, (bf16[2,256,256]{2,1,0:T(8,128)(2,1)S(1)}, ...), branch_computations={%region_41.42_spmd, %region_42.43_spmd} | conditional | flops 269090816 | bytes 6029320
  154.7 13.6 %all-gather = bf16[8,16,512]{2,1,0:T(8,128)(2,1)S(1)} all-gather(bf16[2,16,512]{2,1,0:T(8,128)(2,1)S(1)} %bitcast.1824), channel_id=2, replica_groups=mesh['energy'=4,'rows'=8] {'energy'}, dimensions={0}, use_global_device_ids=true | all-gather | bytes 163840 | tf_op jit(solution)/shard_map/all_gather | solution.py:121
  (258 shorter events, 93.2 us)
Async XLA Ops:
  0.6 153.4 %copy-start = (f32[2]{0:T(128)S(1)}, f32[2]{0:T(128)}, u32[]{:S(2)}) copy-start(f32[2]{0:T(128)} %param.51) | copy-start | bytes 28
  1.7 20.4 %collective-permute-start.4 = (bf16[2,256,256]{2,1,0:T(8,128)(2,1)S(1)}, bf16[2,256,256]{2,1,0:T(8,128)(2,1)S(1)}, u32[]{:S(2)}, u32[]{:S(2)}) collective-permute-start(bf16[2,256,256]{2,1,0:T(8,128)(2,1)S(1)} %constant_dynamic-slice_fusion.1), channel_id=1, source_target_pairs={{0,2},{1,3},{2,0},{3,1},{4,6},{5,7},{6,4},{7,5},{8,10},{9,11},{10,... | collective-permute-start | bytes 786440 | tf_op jit(solution)/shard_map/ppermute | solution.py:11
  4.7 3.2 %collective-permute-start.1 = (bf16[2,256,256]{2,1,0:T(8,128)(2,1)S(1)}, bf16[2,256,256]{2,1,0:T(8,128)(2,1)S(1)}, u32[]{:S(2)}, u32[]{:S(2)}) collective-permute-start(bf16[2,256,256]{2,1,0:T(8,128)(2,1)S(1)} %constant_dynamic-slice_fusion.1), channel_id=1, source_target_pairs={{0,1},{1,0},{2,3},{3,2},{4,5},{5,4},{6,7},{7,6},{8,9},{9,8},{10,11... | collective-permute-start | bytes 786440 | tf_op jit(solution)/shard_map/ppermute | solution.py:11
  6.0 10.7 %collective-permute-start = (bf16[2,256,256]{2,1,0:T(8,128)(2,1)S(1)}, bf16[2,256,256]{2,1,0:T(8,128)(2,1)S(1)}, u32[]{:S(2)}, u32[]{:S(2)}) collective-permute-start(bf16[2,256,256]{2,1,0:T(8,128)(2,1)S(1)} %get-tuple-element.674), channel_id=1, source_target_pairs={{0,2},{1,3},{2,0},{3,1},{4,6},{5,7},{6,4},{7,5},{8,10},{9,11},{10,... | collective-permute-start | bytes 786440 | tf_op jit(solution)/shard_map/ppermute | solution.py:11
  7.4 13.0 %collective-permute-start.7 = (bf16[2,256,256]{2,1,0:T(8,128)(2,1)S(1)}, bf16[2,256,256]{2,1,0:T(8,128)(2,1)S(1)}, u32[]{:S(2)}, u32[]{:S(2)}) collective-permute-start(bf16[2,256,256]{2,1,0:T(8,128)(2,1)S(1)} %pad_maximum_fusion.40), channel_id=1, source_target_pairs={{0,1},{1,0},{2,3},{3,2},{4,5},{5,4},{6,7},{7,6},{8,9},{9,8},{10,11... | collective-permute-start | bytes 786440 | tf_op jit(solution)/shard_map/ppermute | solution.py:11
  18.2 3.8 %collective-permute-start.3 = (bf16[2,256,256]{2,1,0:T(8,128)(2,1)S(1)}, bf16[2,256,256]{2,1,0:T(8,128)(2,1)S(1)}, u32[]{:S(2)}, u32[]{:S(2)}) collective-permute-start(bf16[2,256,256]{2,1,0:T(8,128)(2,1)S(1)} %get-tuple-element.678), channel_id=1, source_target_pairs={{0,1},{1,0},{2,3},{3,2},{4,5},{5,4},{6,7},{7,6},{8,9},{9,8},{10,11... | collective-permute-start | bytes 786440 | tf_op jit(solution)/shard_map/ppermute | solution.py:11
  18.3 9.3 %collective-permute-start.2 = (bf16[2,256,256]{2,1,0:T(8,128)(2,1)S(1)}, bf16[2,256,256]{2,1,0:T(8,128)(2,1)}, u32[]{:S(2)}, u32[]{:S(2)}) collective-permute-start(bf16[2,256,256]{2,1,0:T(8,128)(2,1)S(1)} %pad_maximum_fusion.40), channel_id=1, source_target_pairs={{0,2},{1,3},{2,0},{3,1},{4,6},{5,7},{6,4},{7,5},{8,10},{9,11},{10,... | collective-permute-start | bytes 786440 | tf_op jit(solution)/shard_map/ppermute | solution.py:11
  20.1 13.0 %collective-permute-start.5 = (bf16[2,256,256]{2,1,0:T(8,128)(2,1)S(1)}, bf16[2,256,256]{2,1,0:T(8,128)(2,1)S(1)}, u32[]{:S(2)}, u32[]{:S(2)}) collective-permute-start(bf16[2,256,256]{2,1,0:T(8,128)(2,1)S(1)} %get-tuple-element.673), channel_id=1, source_target_pairs={{0,2},{1,3},{2,0},{3,1},{4,6},{5,7},{6,4},{7,5},{8,10},{9,11},{10,... | collective-permute-start | bytes 786440 | tf_op jit(solution)/shard_map/ppermute | solution.py:11
  22.0 5.7 %collective-permute-start.8 = (bf16[2,256,256]{2,1,0:T(8,128)(2,1)S(1)}, bf16[2,256,256]{2,1,0:T(8,128)(2,1)S(1)}, u32[]{:S(2)}, u32[]{:S(2)}) collective-permute-start(bf16[2,256,256]{2,1,0:T(8,128)(2,1)S(1)} %get-tuple-element.682), channel_id=1, source_target_pairs={{0,1},{1,0},{2,3},{3,2},{4,5},{5,4},{6,7},{7,6},{8,9},{9,8},{10,11... | collective-permute-start | bytes 786440 | tf_op jit(solution)/shard_map/ppermute | solution.py:11
  23.7 9.5 %collective-permute-start.6 = (bf16[2,256,256]{2,1,0:T(8,128)(2,1)S(1)}, bf16[2,256,256]{2,1,0:T(8,128)(2,1)S(1)}, u32[]{:S(2)}, u32[]{:S(2)}) collective-permute-start(bf16[2,256,256]{2,1,0:T(8,128)(2,1)S(1)} %get-tuple-element.680), channel_id=1, source_target_pairs={{0,1},{1,0},{2,3},{3,2},{4,5},{5,4},{6,7},{7,6},{8,9},{9,8},{10,11... | collective-permute-start | bytes 786440 | tf_op jit(solution)/shard_map/ppermute | solution.py:11
  24.2 14.6 %collective-permute-start.11 = (bf16[2,256,256]{2,1,0:T(8,128)(2,1)S(1)}, bf16[2,256,256]{2,1,0:T(8,128)(2,1)}, u32[]{:S(2)}, u32[]{:S(2)}) collective-permute-start(bf16[2,256,256]{2,1,0:T(8,128)(2,1)S(1)} %get-tuple-element.680), channel_id=1, source_target_pairs={{0,2},{1,3},{2,0},{3,1},{4,6},{5,7},{6,4},{7,5},{8,10},{9,11},{10,... | collective-permute-start | bytes 786440 | tf_op jit(solution)/shard_map/ppermute | solution.py:11
  32.8 4.3 %collective-permute-start.14 = (bf16[2,256,256]{2,1,0:T(8,128)(2,1)S(1)}, bf16[2,256,256]{2,1,0:T(8,128)(2,1)S(1)}, u32[]{:S(2)}, u32[]{:S(2)}) collective-permute-start(bf16[2,256,256]{2,1,0:T(8,128)(2,1)S(1)} %get-tuple-element.683), channel_id=1, source_target_pairs={{0,1},{1,0},{2,3},{3,2},{4,5},{5,4},{6,7},{7,6},{8,9},{9,8},{10,11... | collective-permute-start | bytes 786440 | tf_op jit(solution)/shard_map/ppermute | solution.py:11
  34.7 4.1 %collective-permute-start.10 = (bf16[2,256,256]{2,1,0:T(8,128)(2,1)S(1)}, bf16[2,256,256]{2,1,0:T(8,128)(2,1)S(1)}, u32[]{:S(2)}, u32[]{:S(2)}) collective-permute-start(bf16[2,256,256]{2,1,0:T(8,128)(2,1)S(1)} %get-tuple-element.681), channel_id=1, source_target_pairs={{0,1},{1,0},{2,3},{3,2},{4,5},{5,4},{6,7},{7,6},{8,9},{9,8},{10,11... | collective-permute-start | bytes 786440 | tf_op jit(solution)/shard_map/ppermute | solution.py:11
  35.1 20.2 %collective-permute-start.12 = (bf16[2,256,256]{2,1,0:T(8,128)(2,1)S(1)}, bf16[2,256,256]{2,1,0:T(8,128)(2,1)S(1)}, u32[]{:S(2)}, u32[]{:S(2)}) collective-permute-start(bf16[2,256,256]{2,1,0:T(8,128)(2,1)S(1)} %get-tuple-element.675), channel_id=1, source_target_pairs={{0,2},{1,3},{2,0},{3,1},{4,6},{5,7},{6,4},{7,5},{8,10},{9,11},{10,... | collective-permute-start | bytes 786440 | tf_op jit(solution)/shard_map/ppermute | solution.py:11
  36.8 13.1 %collective-permute-start.9 = (bf16[2,256,256]{2,1,0:T(8,128)(2,1)S(1)}, bf16[2,256,256]{2,1,0:T(8,128)(2,1)}, u32[]{:S(2)}, u32[]{:S(2)}) collective-permute-start(bf16[2,256,256]{2,1,0:T(8,128)(2,1)S(1)} %get-tuple-element.683), channel_id=1, source_target_pairs={{0,2},{1,3},{2,0},{3,1},{4,6},{5,7},{6,4},{7,5},{8,10},{9,11},{10,... | collective-permute-start | bytes 786440 | tf_op jit(solution)/shard_map/ppermute | solution.py:11
  38.7 11.3 %collective-permute-start.15 = (bf16[2,256,256]{2,1,0:T(8,128)(2,1)S(1)}, bf16[2,256,256]{2,1,0:T(8,128)(2,1)S(1)}, u32[]{:S(2)}, u32[]{:S(2)}) collective-permute-start(bf16[2,256,256]{2,1,0:T(8,128)(2,1)S(1)} %get-tuple-element.687), channel_id=1, source_target_pairs={{0,1},{1,0},{2,3},{3,2},{4,5},{5,4},{6,7},{7,6},{8,9},{9,8},{10,11... | collective-permute-start | bytes 786440 | tf_op jit(solution)/shard_map/ppermute | solution.py:11
  44.0 11.3 %collective-permute-start.13 = (bf16[2,256,256]{2,1,0:T(8,128)(2,1)S(1)}, bf16[2,256,256]{2,1,0:T(8,128)(2,1)}, u32[]{:S(2)}, u32[]{:S(2)}) collective-permute-start(bf16[2,256,256]{2,1,0:T(8,128)(2,1)S(1)} %get-tuple-element.685), channel_id=1, source_target_pairs={{0,1},{1,0},{2,3},{3,2},{4,5},{5,4},{6,7},{7,6},{8,9},{9,8},{10,11... | collective-permute-start | bytes 786440 | tf_op jit(solution)/shard_map/ppermute | solution.py:11
  44.5 29.3 %collective-permute-start.18 = (bf16[2,256,256]{2,1,0:T(8,128)(2,1)S(1)}, bf16[2,256,256]{2,1,0:T(8,128)(2,1)}, u32[]{:S(2)}, u32[]{:S(2)}) collective-permute-start(bf16[2,256,256]{2,1,0:T(8,128)(2,1)S(1)} %get-tuple-element.685), channel_id=1, source_target_pairs={{0,2},{1,3},{2,0},{3,1},{4,6},{5,7},{6,4},{7,5},{8,10},{9,11},{10,... | collective-permute-start | bytes 786440 | tf_op jit(solution)/shard_map/ppermute | solution.py:11
  55.2 12.8 %collective-permute-start.21 = (bf16[2,256,256]{2,1,0:T(8,128)(2,1)S(1)}, bf16[2,256,256]{2,1,0:T(8,128)(2,1)}, u32[]{:S(2)}, u32[]{:S(2)}) collective-permute-start(bf16[2,256,256]{2,1,0:T(8,128)(2,1)S(1)} %get-tuple-element.688), channel_id=1, source_target_pairs={{0,1},{1,0},{2,3},{3,2},{4,5},{5,4},{6,7},{7,6},{8,9},{9,8},{10,11... | collective-permute-start | bytes 786440 | tf_op jit(solution)/shard_map/ppermute | solution.py:11
  60.7 13.2 %collective-permute-start.17 = (bf16[2,256,256]{2,1,0:T(8,128)(2,1)S(1)}, bf16[2,256,256]{2,1,0:T(8,128)(2,1)}, u32[]{:S(2)}, u32[]{:S(2)}) collective-permute-start(bf16[2,256,256]{2,1,0:T(8,128)(2,1)S(1)} %get-tuple-element.686), channel_id=1, source_target_pairs={{0,1},{1,0},{2,3},{3,2},{4,5},{5,4},{6,7},{7,6},{8,9},{9,8},{10,11... | collective-permute-start | bytes 786440 | tf_op jit(solution)/shard_map/ppermute | solution.py:11
  61.2 34.4 %collective-permute-start.19 = (bf16[2,256,256]{2,1,0:T(8,128)(2,1)S(1)}, bf16[2,256,256]{2,1,0:T(8,128)(2,1)S(1)}, u32[]{:S(2)}, u32[]{:S(2)}) collective-permute-start(bf16[2,256,256]{2,1,0:T(8,128)(2,1)S(1)} %get-tuple-element.672), channel_id=1, source_target_pairs={{0,2},{1,3},{2,0},{3,1},{4,6},{5,7},{6,4},{7,5},{8,10},{9,11},{10,... | collective-permute-start | bytes 786440 | tf_op jit(solution)/shard_map/ppermute | solution.py:11
  64.9 0.7 copy-start.4
  67.5 17.3 %collective-permute-start.16 = (bf16[2,256,256]{2,1,0:T(8,128)(2,1)S(1)}, bf16[2,256,256]{2,1,0:T(8,128)(2,1)}, u32[]{:S(2)}, u32[]{:S(2)}) collective-permute-start(bf16[2,256,256]{2,1,0:T(8,128)(2,1)S(1)} %get-tuple-element.688), channel_id=1, source_target_pairs={{0,2},{1,3},{2,0},{3,1},{4,6},{5,7},{6,4},{7,5},{8,10},{9,11},{10,... | collective-permute-start | bytes 786440 | tf_op jit(solution)/shard_map/ppermute | solution.py:11
  73.9 11.0 %collective-permute-start.22 = (bf16[2,256,256]{2,1,0:T(8,128)(2,1)}, bf16[2,256,256]{2,1,0:T(8,128)(2,1)}, u32[]{:S(2)}, u32[]{:S(2)}) collective-permute-start(bf16[2,256,256]{2,1,0:T(8,128)(2,1)} %get-tuple-element.692), channel_id=1, source_target_pairs={{0,1},{1,0},{2,3},{3,2},{4,5},{5,4},{6,7},{7,6},{8,9},{9,8},{10,11... | collective-permute-start | bytes 786440 | tf_op jit(solution)/shard_map/ppermute | solution.py:11
  79.3 16.3 %collective-permute-start.20 = (bf16[2,256,256]{2,1,0:T(8,128)(2,1)S(1)}, bf16[2,256,256]{2,1,0:T(8,128)(2,1)S(1)}, u32[]{:S(2)}, u32[]{:S(2)}) collective-permute-start(bf16[2,256,256]{2,1,0:T(8,128)(2,1)S(1)} %get-tuple-element.690), channel_id=1, source_target_pairs={{0,1},{1,0},{2,3},{3,2},{4,5},{5,4},{6,7},{7,6},{8,9},{9,8},{10,11... | collective-permute-start | bytes 786440 | tf_op jit(solution)/shard_map/ppermute | solution.py:11
  83.3 1.6 copy-start.5
  94.0 21.8 %collective-permute-start.26 = (bf16[2,256,256]{2,1,0:T(8,128)(2,1)S(1)}, bf16[2,256,256]{2,1,0:T(8,128)(2,1)}, u32[]{:S(2)}, u32[]{:S(2)}) collective-permute-start(bf16[2,256,256]{2,1,0:T(8,128)(2,1)S(1)} %get-tuple-element.693), channel_id=1, source_target_pairs={{0,1},{1,0},{2,3},{3,2},{4,5},{5,4},{6,7},{7,6},{8,9},{9,8},{10,11... | collective-permute-start | bytes 786440 | tf_op jit(solution)/shard_map/ppermute | solution.py:11
  94.1 30.4 %collective-permute-start.23 = (bf16[2,256,256]{2,1,0:T(8,128)(2,1)S(1)}, bf16[2,256,256]{2,1,0:T(8,128)(2,1)}, u32[]{:S(2)}, u32[]{:S(2)}) collective-permute-start(bf16[2,256,256]{2,1,0:T(8,128)(2,1)S(1)} %get-tuple-element.693), channel_id=1, source_target_pairs={{0,2},{1,3},{2,0},{3,1},{4,6},{5,7},{6,4},{7,5},{8,10},{9,11},{10,... | collective-permute-start | bytes 786440 | tf_op jit(solution)/shard_map/ppermute | solution.py:11
  97.2 27.3 %collective-permute-start.24 = (bf16[2,256,256]{2,1,0:T(8,128)(2,1)S(1)}, bf16[2,256,256]{2,1,0:T(8,128)(2,1)}, u32[]{:S(2)}, u32[]{:S(2)}) collective-permute-start(bf16[2,256,256]{2,1,0:T(8,128)(2,1)S(1)} %get-tuple-element.691), channel_id=1, source_target_pairs={{0,1},{1,0},{2,3},{3,2},{4,5},{5,4},{6,7},{7,6},{8,9},{9,8},{10,11... | collective-permute-start | bytes 786440 | tf_op jit(solution)/shard_map/ppermute | solution.py:11
  108.8 31.8 %collective-permute-start.25 = (bf16[2,256,256]{2,1,0:T(8,128)(2,1)S(1)}, bf16[2,256,256]{2,1,0:T(8,128)(2,1)S(1)}, u32[]{:S(2)}, u32[]{:S(2)}) collective-permute-start(bf16[2,256,256]{2,1,0:T(8,128)(2,1)S(1)} %get-tuple-element.690), channel_id=1, source_target_pairs={{0,2},{1,3},{2,0},{3,1},{4,6},{5,7},{6,4},{7,5},{8,10},{9,11},{10,... | collective-permute-start | bytes 786440 | tf_op jit(solution)/shard_map/ppermute | solution.py:11
  121.0 24.9 %collective-permute-start.27 = (bf16[2,256,256]{2,1,0:T(8,128)(2,1)S(1)}, bf16[2,256,256]{2,1,0:T(8,128)(2,1)S(1)}, u32[]{:S(2)}, u32[]{:S(2)}) collective-permute-start(bf16[2,256,256]{2,1,0:T(8,128)(2,1)S(1)} %get-tuple-element.696), channel_id=1, source_target_pairs={{0,1},{1,0},{2,3},{3,2},{4,5},{5,4},{6,7},{7,6},{8,9},{9,8},{10,11... | collective-permute-start | bytes 786440 | tf_op jit(solution)/shard_map/ppermute | solution.py:11
  124.5 6.5 %copy-start.1 = (f32[2,256,256]{2,1,0:T(8,128)S(1)}, f32[2,256,256]{2,1,0:T(8,128)}, u32[]{:S(2)}) copy-start(f32[2,256,256]{2,1,0:T(8,128)} %get-tuple-element.689) | copy-start | bytes 1572868
  133.7 18.0 %all-to-all-start = ((bf16[8,1,2,16,256]{4,3,2,1,0:T(8,128)(2,1)}), bf16[8,1,2,16,256]{4,3,2,1,0:T(8,128)(2,1)S(1)}, u32[]{:S(2)}, u32[]{:S(2)}) async-start(bf16[8,1,2,16,256]{4,3,2,1,0:T(8,128)(2,1)} %copy.23), calls=%async_computation | async-start | bytes 262144 | tf_op jit(solution)/shard_map/all_to_all | solution.py:107
  145.8 0.7 copy-start.2
  151.7 0.7 copy-start.3
